TPU v7x, 128 devices: a whole 4x4x4 slice. The times are simulated.
128 devices in a mesh: brick: 8 (over y, core), grp: 16 (over x, z).
Axes of the slice: x: 4, y: 4, z: 4, core: 2. Of those that a mesh axis runs over, the one named last changes fastest.
Arguments:
- source: float32 [16, 8, 2, 32, 1024], P('grp', 'brick'), may hold values from -21 to 21
- uptake: float32 [16, 8, 2, 32, 1024], P('grp', 'brick'), may hold values from 0.00015 to 0.006
- conductance: float32 [16, 8, 6, 2, 32, 1024], P('grp', 'brick'), may hold values from 0 to 3, as said below
- occupancy: int32 [16, 2, 8], replicated, may hold values from 0 to 1, as said below
- assignment: int32 [8], replicated, may hold values from 0 to 7, as said below
Outputs:
- solution_field: float32 [16, 8, 2, 32, 1024], P('grp', 'brick')
- residual: float32 [16, 8, 2, 32, 1024], P('grp', 'brick')
Inputs may be any that keep to these rules, and one draw needn't show every extreme that they name: `occupancy`: 1 marks an occupied brick; in every draw one patch of some slab has all its bricks occupied. `assignment`: each patch is held by exactly one index of brick. `conductance`: equal at both ends of a bond: the value toward +x at a cell is the value toward -x at its +x neighbour, likewise for y and z, the lattice being read cyclically; values toward +z and -z are 0.3 or more.
All inputs are finite; a program needn't handle non-finite values.
Results may differ from a plain program's by a relative error of at most 0.0003.
Values sent between devices are 32-bit elements; how exact they have to be, the bound alone decides.
A program may use at most 128 MiB of HBM per device.

v0:
```python
import jax
import jax.numpy as jnp
from jax import lax
from jax.sharding import PartitionSpec as P

BS = 32
PATCH_X = 1
PATCH_Y = 2
ITERS = 3
OMEGA = 0.6


def extended_2(block, sides, width):
    for axis, dim in sides:
        count = lax.axis_size(axis)
        forward = [(i, i + 1) for i in range(count - 1)]
        backward = [(target, source) for source, target in forward]
        low = lax.ppermute(
            lax.slice_in_dim(block, block.shape[dim] - width, None, axis=dim), axis, forward
        )
        high = lax.ppermute(lax.slice_in_dim(block, 0, width, axis=dim), axis, backward)
        block = jnp.concatenate([low, block, high], axis=dim)
    return block


def assemble(coarse_diag, couplings, strides):
    extent = coarse_diag.shape[0]
    matrix = jnp.diag(coarse_diag)
    for coupling, stride in zip(couplings, strides):
        banded = coupling[: extent - stride]
        matrix = matrix - jnp.diag(banded, stride) - jnp.diag(banded, -stride)
    return matrix


def pad_rows(block, capacity):
    return jnp.pad(block, ((0, capacity - block.shape[0]), (0, 0)))


def on_device(source, uptake, conductance, occupancy, assignment):
    face_size = BS * BS
    capacity = max(PATCH_X, PATCH_Y)
    slot_count = PATCH_X * PATCH_Y
    slab_index = lax.axis_index("grp")
    brick_index = lax.axis_index("brick")
    brick_count = lax.axis_size("brick")
    across = brick_count // 2
    peer_ids = jnp.arange(brick_count, dtype=jnp.int32)
    patch_index = assignment[brick_index]
    patch_row = patch_index // across
    patch_column = patch_index % across

    def owner_of(row_shift, column_shift):
        row_target = patch_row + row_shift
        column_target = patch_column + column_shift
        inside = (
            (row_target >= 0) & (row_target < 2) & (column_target >= 0) & (column_target < across)
        )
        holder = jnp.sum(jnp.where(assignment == row_target * across + column_target, peer_ids, 0))
        return jnp.where(inside, holder, -1)

    wanted = jnp.stack([owner_of(1, 0), owner_of(-1, 0), owner_of(0, 1), owner_of(0, -1)])
    padded = jnp.pad(occupancy, 1)
    window = lax.dynamic_slice(
        padded,
        (slab_index, patch_row * PATCH_X, patch_column * PATCH_Y),
        (3, PATCH_X + 2, PATCH_Y + 2),
    ).astype(jnp.float32)
    centre = window[1, 1:-1, 1:-1].reshape(slot_count)
    toward = [
        window[1, 2:, 1:-1],
        window[1, :-2, 1:-1],
        window[1, 1:-1, 2:],
        window[1, 1:-1, :-2],
        window[2, 1:-1, 1:-1],
        window[0, 1:-1, 1:-1],
    ]
    first_axis = lax.broadcasted_iota(jnp.int32, (1, BS, face_size), 1)
    flat_axis = lax.broadcasted_iota(jnp.int32, (1, BS, face_size), 2)
    second_axis = flat_axis // BS
    third_axis = flat_axis % BS
    cube_third = lax.broadcasted_iota(jnp.int32, (1, BS, BS, BS), 3)
    borders = [
        first_axis == BS - 1,
        first_axis == 0,
        second_axis == BS - 1,
        second_axis == 0,
        third_axis == BS - 1,
        third_axis == 0,
    ]
    bonds = conductance[0, 0]
    live_here = centre[:, None, None]
    effective = []
    for direction in range(6):
        neighbour_live = toward[direction].reshape(slot_count)[:, None, None]
        active = jnp.where(borders[direction], live_here * neighbour_live, live_here)
        effective.append(bonds[direction] * active)
    absorb = uptake[0, 0]
    diagonal = absorb
    for direction in range(6):
        diagonal = diagonal + effective[direction]

    def apply_operator(field):
        lower_x = field[:, 0, :]
        upper_x = field[:, BS - 1, :]
        lower_y = field[:, :, :BS].reshape(slot_count, face_size)
        upper_y = field[:, :, face_size - BS :].reshape(slot_count, face_size)
        cube = field.reshape(slot_count, BS, BS, BS)
        lower_z = cube[:, :, :, 0].reshape(slot_count, face_size)
        upper_z = cube[:, :, :, BS - 1].reshape(slot_count, face_size)
        grid_lower_x = lower_x.reshape(PATCH_X, PATCH_Y, face_size)
        grid_upper_x = upper_x.reshape(PATCH_X, PATCH_Y, face_size)
        grid_lower_y = lower_y.reshape(PATCH_X, PATCH_Y, face_size)
        grid_upper_y = upper_y.reshape(PATCH_X, PATCH_Y, face_size)
        outgoing_sides = jnp.stack(
            [
                pad_rows(grid_lower_x[0], capacity),
                pad_rows(grid_upper_x[PATCH_X - 1], capacity),
                pad_rows(grid_lower_y[:, 0], capacity),
                pad_rows(grid_upper_y[:, PATCH_Y - 1], capacity),
            ]
        )
        portion = lax.all_gather(outgoing_sides[None], "brick", axis=0, tiled=True)
        sources = jnp.arange(portion.shape[0], dtype=jnp.int32)
        matches = sources[:, None] == wanted[None, :]
        remote = jnp.zeros((4, capacity, face_size), jnp.float32) + jnp.sum(
            jnp.where(matches[:, :, None, None], portion, 0.0), axis=0
        )
        stacked = jnp.stack([lower_z, upper_z])
        extended = extended_2(stacked, (("grp", 0),), 1)
        from_below = extended[0].reshape(slot_count, BS, BS, 1)
        from_above = extended[3].reshape(slot_count, BS, BS, 1)
        beyond_xplus = jnp.concatenate(
            [grid_lower_x[1:], remote[0, :PATCH_Y][None]], axis=0
        ).reshape(slot_count, face_size)
        beyond_xminus = jnp.concatenate(
            [remote[1, :PATCH_Y][None], grid_upper_x[:-1]], axis=0
        ).reshape(slot_count, face_size)
        beyond_yplus = jnp.concatenate(
            [grid_lower_y[:, 1:], remote[2, :PATCH_X][:, None]], axis=1
        ).reshape(slot_count, BS, BS)
        beyond_yminus = jnp.concatenate(
            [remote[3, :PATCH_X][:, None], grid_upper_y[:, :-1]], axis=1
        ).reshape(slot_count, BS, BS)
        upper_neighbour = jnp.where(
            cube_third == BS - 1, from_above, jnp.roll(cube, -1, axis=3)
        ).reshape(slot_count, BS, face_size)
        lower_neighbour = jnp.where(cube_third == 0, from_below, jnp.roll(cube, 1, axis=3)).reshape(
            slot_count, BS, face_size
        )
        total = diagonal * field
        total = total - effective[0] * jnp.concatenate(
            [field[:, 1:, :], beyond_xplus[:, None, :]], axis=1
        )
        total = total - effective[1] * jnp.concatenate(
            [beyond_xminus[:, None, :], field[:, :-1, :]], axis=1
        )
        total = total - effective[2] * jnp.concatenate([field[:, :, BS:], beyond_yplus], axis=2)
        total = total - effective[3] * jnp.concatenate(
            [beyond_yminus, field[:, :, : face_size - BS]], axis=2
        )
        total = total - effective[4] * upper_neighbour
        total = total - effective[5] * lower_neighbour
        return total

    slot_ids = jnp.arange(slot_count)
    brick_first = slot_ids // PATCH_Y
    brick_second = slot_ids % PATCH_Y
    inside = [
        (brick_first < PATCH_X - 1).astype(jnp.float32),
        (brick_first > 0).astype(jnp.float32),
        (brick_second < PATCH_Y - 1).astype(jnp.float32),
        (brick_second > 0).astype(jnp.float32),
    ]
    face_sums = [
        jnp.sum(effective[0][:, BS - 1, :], axis=1),
        jnp.sum(effective[1][:, 0, :], axis=1),
        jnp.sum(effective[2][:, :, face_size - BS :], axis=(1, 2)),
        jnp.sum(effective[3][:, :, :BS], axis=(1, 2)),
        jnp.sum(effective[4].reshape(slot_count, BS, BS, BS)[:, :, :, BS - 1], axis=(1, 2)),
        jnp.sum(effective[5].reshape(slot_count, BS, BS, BS)[:, :, :, 0], axis=(1, 2)),
    ]
    coarse_diag = jnp.sum(absorb, axis=(1, 2))
    for direction in range(4):
        coarse_diag = coarse_diag + face_sums[direction] * inside[direction]
    coarse_diag = coarse_diag + face_sums[4] + face_sums[5]
    grp_count = lax.axis_size("grp")
    grp_ids = jnp.arange(grp_count, dtype=jnp.int32)

    def butterfly(values, axes):
        for axis in axes:
            count = lax.axis_size(axis)
            if count & count - 1:
                values = lax.psum(values, axis)
                continue
            stride = 1
            while stride < count:
                pairs = [(i, i ^ stride) for i in range(count)]
                values = values + lax.ppermute(values, axis, pairs)
                stride *= 2
        return values

    def slab_slot(values):
        here = (grp_ids == slab_index).astype(jnp.float32)
        return here[:, None, None] * values[None]

    forcing = source[0, 0] * live_here
    record = jnp.stack(
        [
            coarse_diag,
            face_sums[0] * inside[0],
            face_sums[2] * inside[2],
            face_sums[4],
            jnp.sum(forcing, axis=(1, 2)),
        ]
    )
    gathered = butterfly(slab_slot(record), ("grp",))
    columns = jnp.transpose(gathered, (1, 0, 2)).reshape(5, -1)
    matrix = assemble(columns[0], (columns[1], columns[2], columns[3]), (PATCH_Y, 1, slot_count))
    factor = jnp.linalg.cholesky(matrix)

    def coarse_solve(terms):
        middle = lax.linalg.triangular_solve(factor, terms[:, None], left_side=True, lower=True)
        result = lax.linalg.triangular_solve(
            factor, middle, left_side=True, lower=True, transpose_a=True
        )
        return lax.dynamic_slice_in_dim(result[:, 0], slab_index * slot_count, slot_count)

    def precondition(residual_field, terms):
        smoothed = OMEGA * residual_field / diagonal
        smoothed = smoothed + OMEGA * (residual_field - apply_operator(smoothed)) / diagonal
        return smoothed + coarse_solve(terms)[:, None, None]

    brick_here = (peer_ids == brick_index).astype(jnp.float32)

    def dot_and_sums(product, field):
        sums = slab_slot(jnp.sum(field, axis=(1, 2))[None])[:, 0]
        spread = brick_here[:, None, None] * sums[None]
        packed = jnp.concatenate([jnp.sum(product)[None], spread.reshape(-1)])
        total = butterfly(packed, ("brick", "grp"))
        mine = lax.dynamic_index_in_dim(
            total[1:].reshape(brick_count, -1), brick_index, keepdims=False
        )
        return (total[0], mine)

    def global_sum(values):
        return butterfly(jnp.sum(values)[None], ("brick", "grp"))[0]

    terms = columns[4]
    solution_field = jnp.zeros_like(forcing)
    residual = forcing
    search = precondition(residual, terms)
    energy = global_sum(residual * search)
    for iteration in range(ITERS):
        mapped = apply_operator(search)
        curvature, mapped_terms = dot_and_sums(search * mapped, mapped)
        step_size = energy / curvature
        solution_field = solution_field + step_size * search
        residual = residual - step_size * mapped
        if iteration + 1 < ITERS:
            terms = terms - step_size * mapped_terms
            smoothed = precondition(residual, terms)
            renewed = global_sum(residual * smoothed)
            search = smoothed + renewed / energy * search
            energy = renewed
    return (solution_field[None, None], residual[None, None])


def solution(mesh):
    return jax.shard_map(
        on_device,
        mesh=mesh,
        in_specs=(
            P("grp", "brick", None, None, None),
            P("grp", "brick", None, None, None),
            P("grp", "brick", None, None, None, None),
            P(),
            P(),
        ),
        out_specs=(P("grp", "brick", None, None, None), P("grp", "brick", None, None, None)),
        check_vma=False,
    )
```

profile of v0, /device:TPU:0, one launch (start us, length us, event | category | flops | bytes accessed | tf_op | source)
XLA Modules:
  0.0 795.7 jit_solution(16637626487733563843)
XLA Ops:
  31.3 5.5 multiply_divide_fusion.2
  46.3 2.5 collective-permute-start.1
  62.5 13.4 %all-gather = f32[32,2,1024]{2,1,0:T(2,128)S(1)} all-gather(f32[4,2,1024]{2,1,0:T(2,128)S(1)} %copy.421), channel_id=2, replica_groups=mesh['brick'=8,'grp'=16] {'brick'}, dimensions={0}, use_global_device_ids=true | all-gather | bytes 294912 | tf_op jit(solution)/shard_map/all_gather | solution.py:122
  84.2 5.6 collective-permute-start.3
  92.7 3.5 collective-permute-start.4
  102.1 3.0 collective-permute-start.5
  112.6 2.9 cholesky.19
  121.3 8.5 %fusion.46 = (f32[2,32,32,32]{3,2,1,0:T(8,128)S(1)}, f32[2,32,32,32]{3,2,1,0:T(8,128)}, f32[2,32,32,32]{3,2,1,0:T(8,128)}) fusion(f32[2,32,32,32]{3,2,1,0:T(8,128)} %get-tuple-element.73, f32[2,32,32,32]{3,2,1,0:T(8,128)} %copy-done.15, f32[2,32,32,32]{3,2,1,0:T(8,128)} %copy-done.14, f32[2,32,32,32]{3,2,1,0:T(8,128)} %concatenate.668, ...), kind=kLoop, calls=%fused_computation.88 | loop fusion | flops 2293760 | bytes 4538480 | tf_op jit(solution)/shard_map/add | solution.py:231
  152.9 12.8 %all-gather.1 = f32[32,2,1024]{2,1,0:T(2,128)S(1)} all-gather(f32[4,2,1024]{2,1,0:T(2,128)S(1)} %copy.424), channel_id=3, replica_groups=mesh['brick'=8,'grp'=16] {'brick'}, dimensions={0}, use_global_device_ids=true | all-gather | bytes 294912 | tf_op jit(solution)/shard_map/all_gather | solution.py:122
  181.4 3.0 pad_maximum_fusion.2
  206.9 3.8 multiply_reduce_fusion.4
  222.3 3.2 collective-permute-done.17
  225.5 2.6 collective-permute-start.18
  229.7 3.5 collective-permute-start.19
  235.4 4.4 collective-permute-start.20
  254.8 2.7 collective-permute-start.7
  259.0 3.3 collective-permute-start.8
  270.3 3.7 collective-permute-done.10
  278.8 3.7 collective-permute-start.12
  296.8 13.2 %all-gather.2 = f32[32,2,1024]{2,1,0:T(2,128)S(1)} all-gather(f32[4,2,1024]{2,1,0:T(2,128)S(1)} %copy.430), channel_id=4, replica_groups=mesh['brick'=8,'grp'=16] {'brick'}, dimensions={0}, use_global_device_ids=true | all-gather | bytes 294912 | tf_op jit(solution)/shard_map/all_gather | solution.py:122
  315.7 6.9 multiply_divide_fusion.1
  332.4 2.5 collective-permute-start.23
  338.7 3.0 pad_maximum_fusion.4
  372.2 3.8 multiply_reduce_fusion.3
  381.9 2.7 collective-permute-start.25
  386.1 3.3 collective-permute-start.26
  391.8 4.0 collective-permute-start.27
  396.5 3.8 collective-permute-start.28
  402.3 5.7 collective-permute-start.29
  408.8 4.9 collective-permute-start.30
  417.2 13.0 %all-gather.3 = f32[32,2,1024]{2,1,0:T(2,128)S(1)} all-gather(f32[4,2,1024]{2,1,0:T(2,128)S(1)} %copy.435), channel_id=5, replica_groups=mesh['brick'=8,'grp'=16] {'brick'}, dimensions={0}, use_global_device_ids=true | all-gather | bytes 294912 | tf_op jit(solution)/shard_map/all_gather | solution.py:122
  434.1 6.3 multiply_add_fusion.1
  447.6 2.7 pad_maximum_fusion.6
  467.3 3.4 multiply_reduce_fusion.2
  479.1 3.2 collective-permute-done.35
  482.3 2.6 collective-permute-start.36
  486.5 4.1 collective-permute-start.37
  492.2 5.5 collective-permute-start.38
  499.9 3.6 collective-permute-start.39
  517.4 13.1 %all-gather.4 = f32[32,2,1024]{2,1,0:T(2,128)S(1)} all-gather(f32[4,2,1024]{2,1,0:T(2,128)S(1)} %copy.440), channel_id=6, replica_groups=mesh['brick'=8,'grp'=16] {'brick'}, dimensions={0}, use_global_device_ids=true | all-gather | bytes 294912 | tf_op jit(solution)/shard_map/all_gather | solution.py:122
  535.4 6.6 multiply_divide_fusion
  556.8 3.1 pad_maximum_fusion.8
  589.0 3.9 multiply_reduce_fusion.1
  598.7 2.6 collective-permute-start.43
  603.1 3.3 collective-permute-start.44
  608.9 4.0 collective-permute-start.45
  613.9 3.0 collective-permute-start.46
  619.7 4.9 collective-permute-start.47
  625.6 4.0 collective-permute-start.48
  641.0 13.2 %all-gather.5 = f32[32,2,1024]{2,1,0:T(2,128)S(1)} all-gather(f32[4,2,1024]{2,1,0:T(2,128)S(1)} %copy.445), channel_id=7, replica_groups=mesh['brick'=8,'grp'=16] {'brick'}, dimensions={0}, use_global_device_ids=true | all-gather | bytes 294912 | tf_op jit(solution)/shard_map/all_gather | solution.py:122
  659.3 9.3 %multiply_add_fusion = f32[2,32,32,32]{3,2,1,0:T(8,128)S(1)} fusion(f32[2,32,32,32]{3,2,1,0:T(8,128)} %copy-done.16, f32[2,32,32,32]{3,2,1,0:T(8,128)} %get-tuple-element.73, f32[2,32,32,32]{3,2,1,0:T(8,128)} %copy-done.15, f32[2,32,32,32]{3,2,1,0:T(8,128)} %copy-done.14, f32[2,32,32,32]{3,2,1,0:T(8,128)} %concatenate.784, ...), kind=kLoop, calls=%fused_computation.76 | loop fusion | flops 3735552 | bytes 5865592 | tf_op jit(solution)/shard_map/add | solution.py:263
  686.7 2.6 broadcast_in_dim.796
  706.1 3.2 collective-permute-done.53
  709.3 2.6 collective-permute-start.54
  713.5 3.8 collective-permute-start.55
  723.7 2.5 broadcast_in_dim.759
  731.3 2.5 concatenate.738
  740.0 3.9 fusion.96
  751.7 2.8 collective-permute-start.57
  764.3 2.5 broadcast_in_dim.799
  771.9 2.5 concatenate.817
  775.6 2.5 broadcast_in_dim.800
  783.1 2.5 broadcast_in_dim.803
  788.8 5.9 fusion.148
  (938 shorter events, 469.3 us)
Async XLA Ops:
  5.1 100.0 %copy-start.121 = (pred[32]{0:T(512)(128)(4,1)}, pred[32]{0:T(512)(128)(4,1)S(1)}, u32[]{:S(2)}) copy-start(pred[32]{0:T(512)(128)(4,1)S(1)} %get-tuple-element.280) | copy-start | bytes 100
  5.1 100.6 %copy-start.127 = (pred[32]{0:T(512)(128)(4,1)}, pred[32]{0:T(512)(128)(4,1)S(1)}, u32[]{:S(2)}) copy-start(pred[32]{0:T(512)(128)(4,1)S(1)} %get-tuple-element.281) | copy-start | bytes 100
  15.0 357.2 %copy-start.21 = (f32[2,32,1024]{2,1,0:T(8,128)}, f32[2,32,1024]{2,1,0:T(8,128)S(1)}, u32[]{:S(2)}) copy-start(f32[2,32,1024]{2,1,0:T(8,128)S(1)} %get-tuple-element.70) | copy-start | bytes 786436
  40.5 42.8 %collective-permute-start.2 = (f32[16,5,2]{2,0,1:T(8,128)}, f32[16,5,2]{2,0,1:T(8,128)}, u32[]{:S(2)}, u32[]{:S(2)}) collective-permute-start(f32[16,5,2]{2,0,1:T(8,128)} %broadcast_multiply_fusion.3), channel_id=1, source_target_pairs={{0,1},{1,0},{2,3},{3,2},{4,5},{5,4},{6,7},{7,6},{8,9},{9,8},{10,11... | collective-permute-start | bytes 1928 | tf_op jit(solution)/shard_map/ppermute | solution.py:198
  46.3 74.2 %collective-permute-start.1 = (f32[1,2,1024]{2,1,0:T(2,128)}, f32[1,2,1024]{2,1,0:T(2,128)}, u32[]{:S(2)}, u32[]{:S(2)}) collective-permute-start(f32[1,2,1024]{2,1,0:T(2,128)} %stack_reshape_squeeze.37), channel_id=1, source_target_pairs={{0,1},{1,2},{2,3},{3,4},{4,5},{5,6},{6,7},{7,8},{8,9},{9,10},{10,1... | collective-permute-start | bytes 24584 | tf_op jit(solution)/shard_map/ppermute | solution.py:18
  50.3 69.5 %collective-permute-start = (f32[1,2,1024]{2,1,0:T(2,128)}, f32[1,2,1024]{2,1,0:T(2,128)}, u32[]{:S(2)}, u32[]{:S(2)}) collective-permute-start(f32[1,2,1024]{2,1,0:T(2,128)} %stack_reshape_squeeze.36), channel_id=1, source_target_pairs={{1,0},{2,1},{3,2},{4,3},{5,4},{6,5},{7,6},{8,7},{9,8},{10,9},{11,1... | collective-permute-start | bytes 24584 | tf_op jit(solution)/shard_map/ppermute | solution.py:21
  84.2 7.6 collective-permute-start.3
  92.7 9.4 %collective-permute-start.4 = (f32[16,5,2]{2,0,1:T(8,128)S(1)}, f32[16,5,2]{2,0,1:T(8,128)S(1)}, u32[]{:S(2)}, u32[]{:S(2)}) collective-permute-start(f32[16,5,2]{2,0,1:T(8,128)S(1)} %fusion.258), channel_id=1, source_target_pairs={{0,4},{1,5},{2,6},{3,7},{4,0},{5,1},{6,2},{7,3},{8,12},{9,13},{10,... | collective-permute-start | bytes 1928 | tf_op jit(solution)/shard_map/ppermute | solution.py:198
  102.1 9.6 %collective-permute-start.5 = (f32[16,5,2]{2,0,1:T(8,128)S(1)}, f32[16,5,2]{2,0,1:T(8,128)S(1)}, u32[]{:S(2)}, u32[]{:S(2)}) collective-permute-start(f32[16,5,2]{2,0,1:T(8,128)S(1)} %add.671), channel_id=1, source_target_pairs={{0,8},{1,9},{2,10},{3,11},{4,12},{5,13},{6,14},{7,15},{8,0},{9,1},... | collective-permute-start | bytes 1928 | tf_op jit(solution)/shard_map/ppermute | solution.py:198
  176.7 18.5 %collective-permute-start.14 = (f32[1,2,1024]{2,1,0:T(2,128)}, f32[1,2,1024]{2,1,0:T(2,128)}, u32[]{:S(2)}, u32[]{:S(2)}) collective-permute-start(f32[1,2,1024]{2,1,0:T(2,128)} %stack_reshape_squeeze.39), channel_id=1, source_target_pairs={{0,1},{1,2},{2,3},{3,4},{4,5},{5,6},{6,7},{7,8},{8,9},{9,10},{10,1... | collective-permute-start | bytes 24584 | tf_op jit(solution)/shard_map/ppermute | solution.py:18
  178.6 22.5 %collective-permute-start.13 = (f32[1,2,1024]{2,1,0:T(2,128)}, f32[1,2,1024]{2,1,0:T(2,128)}, u32[]{:S(2)}, u32[]{:S(2)}) collective-permute-start(f32[1,2,1024]{2,1,0:T(2,128)} %stack_reshape_squeeze.38), channel_id=1, source_target_pairs={{1,0},{2,1},{3,2},{4,3},{5,4},{6,5},{7,6},{8,7},{9,8},{10,9},{11,1... | collective-permute-start | bytes 24584 | tf_op jit(solution)/shard_map/ppermute | solution.py:21
  214.3 1.2 collective-permute-start.15
  216.8 3.6 collective-permute-start.16
  220.4 5.1 collective-permute-start.17
  225.5 4.2 collective-permute-start.18
  229.7 5.1 collective-permute-start.19
  235.4 16.3 %collective-permute-start.20 = (f32[257]{0:T(512)}, f32[257]{0:T(512)}, u32[]{:S(2)}, u32[]{:S(2)}) collective-permute-start(f32[257]{0:T(512)} %add.700), channel_id=1, source_target_pairs={{0,4},{1,5},{2,6},{3,7},{4,0},{5,1},{6,2},{7,3},{8,12},{9,13},{10,... | collective-permute-start | bytes 3092 | tf_op jit(solution)/shard_map/ppermute | solution.py:198
  247.0 6.6 collective-permute-start.6
  252.4 32.1 %collective-permute-start.21 = (f32[257]{0:T(512)S(1)}, f32[257]{0:T(512)S(1)}, u32[]{:S(2)}, u32[]{:S(2)}) collective-permute-start(f32[257]{0:T(512)S(1)} %add.701), channel_id=1, source_target_pairs={{0,8},{1,9},{2,10},{3,11},{4,12},{5,13},{6,14},{7,15},{8,0},{9,1},... | collective-permute-start | bytes 3092 | tf_op jit(solution)/shard_map/ppermute | solution.py:198
  254.8 3.6 collective-permute-start.7
  259.0 5.1 collective-permute-start.8
  264.7 3.6 collective-permute-start.9
  268.9 5.1 collective-permute-start.10
  274.6 3.6 collective-permute-start.11
  278.8 5.1 collective-permute-start.12
  332.4 28.0 %collective-permute-start.23 = (f32[1,2,1024]{2,1,0:T(2,128)}, f32[1,2,1024]{2,1,0:T(2,128)}, u32[]{:S(2)}, u32[]{:S(2)}) collective-permute-start(f32[1,2,1024]{2,1,0:T(2,128)} %stack_reshape_squeeze.41), channel_id=1, source_target_pairs={{0,1},{1,2},{2,3},{3,4},{4,5},{5,6},{6,7},{7,8},{8,9},{9,10},{10,1... | collective-permute-start | bytes 24584 | tf_op jit(solution)/shard_map/ppermute | solution.py:18
  334.9 31.4 %collective-permute-start.22 = (f32[1,2,1024]{2,1,0:T(2,128)}, f32[1,2,1024]{2,1,0:T(2,128)}, u32[]{:S(2)}, u32[]{:S(2)}) collective-permute-start(f32[1,2,1024]{2,1,0:T(2,128)} %stack_reshape_squeeze.40), channel_id=1, source_target_pairs={{1,0},{2,1},{3,2},{4,3},{5,4},{6,5},{7,6},{8,7},{9,8},{10,9},{11,1... | collective-permute-start | bytes 24584 | tf_op jit(solution)/shard_map/ppermute | solution.py:21
  375.9 4.7 collective-permute-start.24
  381.9 3.6 collective-permute-start.25
  386.1 5.1 collective-permute-start.26
  391.8 4.1 collective-permute-start.27
  396.5 5.1 collective-permute-start.28
  402.3 5.9 collective-permute-start.29
  408.8 5.1 collective-permute-start.30
  444.3 13.6 %collective-permute-start.32 = (f32[1,2,1024]{2,1,0:T(2,128)S(1)}, f32[1,2,1024]{2,1,0:T(2,128)S(1)}, u32[]{:S(2)}, u32[]{:S(2)}) collective-permute-start(f32[1,2,1024]{2,1,0:T(2,128)S(1)} %stack_reshape_squeeze.43), channel_id=1, source_target_pairs={{0,1},{1,2},{2,3},{3,4},{4,5},{5,6},{6,7},{7,8},{8,9},{9,10},{10,1... | collective-permute-start | bytes 24584 | tf_op jit(solution)/shard_map/ppermute | solution.py:18
  446.3 16.3 %collective-permute-start.31 = (f32[1,2,1024]{2,1,0:T(2,128)}, f32[1,2,1024]{2,1,0:T(2,128)}, u32[]{:S(2)}, u32[]{:S(2)}) collective-permute-start(f32[1,2,1024]{2,1,0:T(2,128)} %stack_reshape_squeeze.42), channel_id=1, source_target_pairs={{1,0},{2,1},{3,2},{4,3},{5,4},{6,5},{7,6},{8,7},{9,8},{10,9},{11,1... | collective-permute-start | bytes 24584 | tf_op jit(solution)/shard_map/ppermute | solution.py:21
  470.7 37.8 %copy-start.76 = (f32[2,31,1024]{2,1,0:T(8,128)S(1)}, f32[2,31,1024]{2,1,0:T(8,128)}, u32[]{:S(2)}) copy-start(f32[2,31,1024]{2,1,0:T(8,128)} %get-tuple-element.133) | copy-start | bytes 761860
  470.7 39.1 %copy-start.82 = (f32[2,32,1024]{2,1,0:T(8,128)S(1)}, f32[2,32,1024]{2,1,0:T(8,128)}, u32[]{:S(2)}) copy-start(f32[2,32,1024]{2,1,0:T(8,128)} %get-tuple-element.50) | copy-start | bytes 786436
  471.7 1.2 collective-permute-start.33
  473.6 3.6 collective-permute-start.34
  477.2 5.1 collective-permute-start.35
  482.3 4.2 collective-permute-start.36
  486.5 5.7 collective-permute-start.37
  492.2 7.1 collective-permute-start.38
  499.9 12.6 %collective-permute-start.39 = (f32[257]{0:T(512)}, f32[257]{0:T(512)}, u32[]{:S(2)}, u32[]{:S(2)}) collective-permute-start(f32[257]{0:T(512)} %add.733), channel_id=1, source_target_pairs={{0,8},{1,9},{2,10},{3,11},{4,12},{5,13},{6,14},{7,15},{8,0},{9,1},... | collective-permute-start | bytes 3092 | tf_op jit(solution)/shard_map/ppermute | solution.py:198
  551.6 25.7 %collective-permute-start.41 = (f32[1,2,1024]{2,1,0:T(2,128)}, f32[1,2,1024]{2,1,0:T(2,128)}, u32[]{:S(2)}, u32[]{:S(2)}) collective-permute-start(f32[1,2,1024]{2,1,0:T(2,128)} %stack_reshape_squeeze.45), channel_id=1, source_target_pairs={{0,1},{1,2},{2,3},{3,4},{4,5},{5,6},{6,7},{7,8},{8,9},{9,10},{10,1... | collective-permute-start | bytes 24584 | tf_op jit(solution)/shard_map/ppermute | solution.py:18
  554.1 29.1 %collective-permute-start.40 = (f32[1,2,1024]{2,1,0:T(2,128)}, f32[1,2,1024]{2,1,0:T(2,128)}, u32[]{:S(2)}, u32[]{:S(2)}) collective-permute-start(f32[1,2,1024]{2,1,0:T(2,128)} %stack_reshape_squeeze.44), channel_id=1, source_target_pairs={{1,0},{2,1},{3,2},{4,3},{5,4},{6,5},{7,6},{8,7},{9,8},{10,9},{11,1... | collective-permute-start | bytes 24584 | tf_op jit(solution)/shard_map/ppermute | solution.py:21
  592.9 4.6 collective-permute-start.42
  595.3 59.0 %copy-start.191 = (pred[8,4]{1,0:T(8,128)(4,1)S(1)}, pred[8,4]{1,0:T(8,128)(4,1)}, u32[]{:S(2)}) copy-start(pred[8,4]{1,0:T(8,128)(4,1)} %copy-done.189) | copy-start | bytes 100
  598.7 3.7 collective-permute-start.43
  603.1 5.2 collective-permute-start.44
  608.9 4.3 collective-permute-start.45
  613.9 5.2 collective-permute-start.46
  619.7 5.3 collective-permute-start.47
  625.6 5.2 collective-permute-start.48
  672.8 12.3 %collective-permute-start.50 = (f32[1,2,1024]{2,1,0:T(2,128)S(1)}, f32[1,2,1024]{2,1,0:T(2,128)S(1)}, u32[]{:S(2)}, u32[]{:S(2)}) collective-permute-start(f32[1,2,1024]{2,1,0:T(2,128)S(1)} %stack_reshape_squeeze.47), channel_id=1, source_target_pairs={{0,1},{1,2},{2,3},{3,4},{4,5},{5,6},{6,7},{7,8},{8,9},{9,10},{10,1... | collective-permute-start | bytes 24584 | tf_op jit(solution)/shard_map/ppermute | solution.py:18
  675.2 14.0 %collective-permute-start.49 = (f32[1,2,1024]{2,1,0:T(2,128)}, f32[1,2,1024]{2,1,0:T(2,128)}, u32[]{:S(2)}, u32[]{:S(2)}) collective-permute-start(f32[1,2,1024]{2,1,0:T(2,128)} %stack_reshape_squeeze.46), channel_id=1, source_target_pairs={{1,0},{2,1},{3,2},{4,3},{5,4},{6,5},{7,6},{8,7},{9,8},{10,9},{11,1... | collective-permute-start | bytes 24584 | tf_op jit(solution)/shard_map/ppermute | solution.py:21
  698.7 1.2 collective-permute-start.51
  700.6 3.6 collective-permute-start.52
  704.2 5.1 collective-permute-start.53
  709.3 4.2 collective-permute-start.54
  713.5 23.9 %collective-permute-start.55 = (f32[257]{0:T(512)S(1)}, f32[257]{0:T(512)S(1)}, u32[]{:S(2)}, u32[]{:S(2)}) collective-permute-start(f32[257]{0:T(512)S(1)} %add.759), channel_id=1, source_target_pairs={{0,2},{1,3},{2,0},{3,1},{4,6},{5,7},{6,4},{7,5},{8,10},{9,11},{10,... | collective-permute-start | bytes 3092 | tf_op jit(solution)/shard_map/ppermute | solution.py:198
  738.0 12.3 %collective-permute-start.56 = (f32[257]{0:T(512)}, f32[257]{0:T(512)}, u32[]{:S(2)}, u32[]{:S(2)}) collective-permute-start(f32[257]{0:T(512)} %add.760), channel_id=1, source_target_pairs={{0,4},{1,5},{2,6},{3,7},{4,0},{5,1},{6,2},{7,3},{8,12},{9,13},{10,... | collective-permute-start | bytes 3092 | tf_op jit(solution)/shard_map/ppermute | solution.py:198
  751.7 35.1 %collective-permute-start.57 = (f32[257]{0:T(512)}, f32[257]{0:T(512)}, u32[]{:S(2)}, u32[]{:S(2)}) collective-permute-start(f32[257]{0:T(512)} %add.761), channel_id=1, source_target_pairs={{0,8},{1,9},{2,10},{3,11},{4,12},{5,13},{6,14},{7,15},{8,0},{9,1},... | collective-permute-start | bytes 3092 | tf_op jit(solution)/shard_map/ppermute | solution.py:198
  (221 other events, 1256.4 us)
where the time goes:
time: 810 us; the launch traced here: 796 us
  local copies, waits for them, and re-layouts  344 us (42%)
  other arithmetic  145 us (18%)
  starting transfers between devices  145 us (18%)
  blocking collectives  78.8 us (10%)
  waiting for transfers between devices  54 us (7%)
  between operations  25.7 us (3%)
    ppermute x46, starting transfers between devices, butterfly(): values = values + lax.ppermute(values, axis, pairs)  124 us
    all_gather x6, blocking collectives, apply_operator(): portion = lax.all_gather(outgoing_sides[None], 'brick', axis=0, tiled=True)  78.8 us
    ppermute x46, waiting for transfers between devices, butterfly(): values = values + lax.ppermute(values, axis, pairs)  54 us
    broadcast_in_dim x26, local copies, waits for them, and re-layouts, apply_operator(): jnp.where(cube_third == BS - 1, from_above, jnp.roll(cube, -1, axis=3))  46.7 us
    broadcast_in_dim x26, local copies, waits for them, and re-layouts, apply_operator(): jnp.where(cube_third == 0, from_below, jnp.roll(cube, 1, axis=3))  42.9 us
    concatenate x12, local copies, waits for them, and re-layouts, apply_operator(): jnp.roll(cube, 1, axis=3)  25.5 us
    concatenate x12, local copies, waits for them, and re-layouts, apply_operator(): jnp.roll(cube, -1, axis=3)  23 us
    concatenate x15, local copies, waits for them, and re-layouts, apply_operator(): jnp.concatenate([field[:, :, BS:], beyond_yplus], axis=2)  21.9 us
  transfers between devices with their start and end apart: 58, of which 34 were waited for; matrix products, arithmetic and copies ran while one was open for 30% of the time, Pallas kernels for 0%

commit v1 on v0

--- a/solution.py
+++ b/solution.py
@@ -8,6 +8,12 @@
 PATCH_Y = 2
 ITERS = 3
 OMEGA = 0.6
+
+
+def gather_by_exchange(x, axis, dim):
+    size = lax.axis_size(axis)
+    repeats = [size if d == dim else 1 for d in range(x.ndim)]
+    return lax.all_to_all(jnp.tile(x, repeats), axis, split_axis=dim, concat_axis=dim, tiled=True)
 
 
 def extended_2(block, sides, width):
@@ -119,7 +125,7 @@
                 pad_rows(grid_upper_y[:, PATCH_Y - 1], capacity),
             ]
         )
-        portion = lax.all_gather(outgoing_sides[None], "brick", axis=0, tiled=True)
+        portion = gather_by_exchange(outgoing_sides[None], "brick", 0)
         sources = jnp.arange(portion.shape[0], dtype=jnp.int32)
         matches = sources[:, None] == wanted[None, :]
         remote = jnp.zeros((4, capacity, face_size), jnp.float32) + jnp.sum(

time: 810 us -> 758 us (0.936)
  blocking collectives: 78.8 us -> 0 us
  starting transfers between devices: 145 us -> 188 us
  local copies, waits for them, and re-layouts: 344 us -> 329 us
  waiting for transfers between devices: 54 us -> 42.6 us
  other arithmetic: 145 us -> 154 us
    all_gather x6 -> x0, blocking collectives: 78.8 us -> none  [apply_operator(): portion = lax.all_gather(outgoing_sides[None], 'brick', axis=0, tiled=True)]
    all_to_all x0 -> x6, starting transfers between devices: none -> 28.6 us  [gather_by_exchange(): lax.all_to_all(jnp.tile(x, repeats), axis, split_axis=dim, concat_axis=di...]
    ppermute x46, starting transfers between devices: 124 us -> 139 us  [butterfly(): values = values + lax.ppermute(values, axis, pairs)]
    ppermute x46, waiting for transfers between devices: 54 us -> 42.6 us  [butterfly(): values = values + lax.ppermute(values, axis, pairs)]
    another operation x0 -> x19, local copies, waits for them, and re-layouts: none -> 11.4 us  [the longest x6 4.7 us: gather_by_exchange(): jnp.tile(x, repeats)]
    concatenate x14 -> x24, local copies, waits for them, and re-layouts: 20.6 us -> 25.5 us  [apply_operator(): jnp.concatenate([field[:, 1:, :], beyond_xplus[:, None, :]], axis=1)]
    concatenate x11 -> x18, local copies, waits for them, and re-layouts: 18.3 us -> 21.5 us  [apply_operator(): jnp.concatenate([beyond_xminus[:, None, :], field[:, :-1, :]], axis=1)]
  transfers between devices with their start and end apart: 58 -> 64, of which waited for: 34 -> 34; matrix products, arithmetic and copies ran while one was open for 30% -> 37% of each run, Pallas kernels for 0% -> 0%
where the time goes in v1:
time: 758 us; the launch traced here: 743 us
  local copies, waits for them, and re-layouts  329 us (43%)
  starting transfers between devices  188 us (25%)
  other arithmetic  154 us (20%)
  waiting for transfers between devices  42.6 us (6%)
  between operations  26.1 us (3%)
    ppermute x46, starting transfers between devices, butterfly(): values = values + lax.ppermute(values, axis, pairs)  139 us
    ppermute x46, waiting for transfers between devices, butterfly(): values = values + lax.ppermute(values, axis, pairs)  42.6 us
    broadcast_in_dim x26, local copies, waits for them, and re-layouts, apply_operator(): jnp.where(cube_third == BS - 1, from_above, jnp.roll(cube, -1, axis=3))  41.1 us
    broadcast_in_dim x26, local copies, waits for them, and re-layouts, apply_operator(): jnp.where(cube_third == 0, from_below, jnp.roll(cube, 1, axis=3))  40.3 us
    all_to_all x6, starting transfers between devices, gather_by_exchange(): lax.all_to_all(jnp.tile(x, repeats), axis, split_axis=dim, concat_axis=di...  28.6 us
    concatenate x24, local copies, waits for them, and re-layouts, apply_operator(): jnp.concatenate([field[:, 1:, :], beyond_xplus[:, None, :]], axis=1)  25.5 us
    concatenate x12, local copies, waits for them, and re-layouts, apply_operator(): jnp.roll(cube, -1, axis=3)  24.2 us
    concatenate x12, local copies, waits for them, and re-layouts, apply_operator(): jnp.roll(cube, 1, axis=3)  24.2 us
  transfers between devices with their start and end apart: 64, of which 34 were waited for; matrix products, arithmetic and copies ran while one was open for 37% of the time, Pallas kernels for 0%

profile of v1, /device:TPU:0, one launch (start us, length us, event | category | flops | bytes accessed | tf_op | source)
XLA Modules:
  0.0 743.1 jit_solution(3704224139463503153)
XLA Ops:
  10.9 4.6 all-to-all-start
  42.1 5.5 multiply_divide_fusion.2
  57.0 2.6 collective-permute-start.1
  71.6 5.6 collective-permute-start.3
  80.0 3.6 collective-permute-start.4
  85.6 3.7 collective-permute-start.5
  94.1 2.9 cholesky.19
  119.4 8.4 %fusion.46 = (f32[2,32,32,32]{3,2,1,0:T(8,128)S(1)}, f32[2,32,32,32]{3,2,1,0:T(8,128)}, f32[2,32,32,32]{3,2,1,0:T(8,128)}) fusion(f32[2,32,32,32]{3,2,1,0:T(8,128)} %get-tuple-element.67, f32[2,32,32,32]{3,2,1,0:T(8,128)} %copy-done.17, f32[2,32,32,32]{3,2,1,0:T(8,128)} %copy-done.16, f32[2,32,32,32]{3,2,1,0:T(8,128)} %concatenate.668, ...), kind=kLoop, calls=%fused_computation.88 | loop fusion | flops 2293760 | bytes 4538480 | tf_op jit(solution)/shard_map/add | solution.py:237
  150.2 4.8 all-to-all-start.1
  161.3 3.0 pad_maximum_fusion.2
  191.2 3.8 multiply_reduce_fusion.4
  204.8 3.4 collective-permute-start.17
  209.9 2.5 collective-permute-start.18
  213.9 3.5 collective-permute-start.19
  219.6 4.7 collective-permute-start.20
  240.4 3.4 collective-permute-start.7
  244.7 4.9 collective-permute-start.8
  256.3 3.8 collective-permute-done.10
  265.1 3.2 collective-permute-start.12
  279.0 6.6 multiply_divide_fusion.1
  300.3 4.8 all-to-all-start.2
  311.8 3.0 pad_maximum_fusion.4
  349.6 3.7 multiply_reduce_fusion.3
  359.5 3.2 collective-permute-start.25
  363.8 4.7 collective-permute-start.26
  369.7 3.8 collective-permute-start.27
  374.5 3.4 collective-permute-start.28
  380.3 5.2 collective-permute-start.29
  386.5 4.7 collective-permute-start.30
  396.1 6.4 multiply_add_fusion.1
  408.0 4.8 all-to-all-start.3
  417.1 2.7 pad_maximum_fusion.6
  435.5 3.4 multiply_reduce_fusion.2
  445.2 3.5 collective-permute-start.35
  450.3 2.6 collective-permute-start.36
  454.5 3.9 collective-permute-start.37
  460.0 5.5 collective-permute-start.38
  467.7 3.4 collective-permute-start.39
  486.7 6.2 multiply_divide_fusion
  504.2 4.8 all-to-all-start.4
  514.5 3.1 pad_maximum_fusion.8
  551.7 3.9 multiply_reduce_fusion.1
  561.7 3.2 collective-permute-start.43
  565.9 4.7 collective-permute-start.44
  571.6 3.8 collective-permute-start.45
  576.2 3.7 collective-permute-start.46
  581.9 5.9 collective-permute-start.47
  588.6 4.4 collective-permute-start.48
  598.3 9.3 %multiply_add_fusion = f32[2,32,32,32]{3,2,1,0:T(8,128)S(1)} fusion(f32[2,32,32,32]{3,2,1,0:T(8,128)} %copy-done.18, f32[2,32,32,32]{3,2,1,0:T(8,128)} %get-tuple-element.67, f32[2,32,32,32]{3,2,1,0:T(8,128)} %copy-done.17, f32[2,32,32,32]{3,2,1,0:T(8,128)} %copy-done.16, f32[2,32,32,32]{3,2,1,0:T(8,128)} %concatenate.784, ...), kind=kLoop, calls=%fused_computation.76 | loop fusion | flops 3735552 | bytes 5865592 | tf_op jit(solution)/shard_map/add | solution.py:269
  613.4 4.8 all-to-all-start.5
  640.3 2.5 multiply_reduce_fusion
  649.4 3.5 collective-permute-start.53
  654.5 2.8 collective-permute-start.54
  659.7 2.5 broadcast_in_dim.741
  667.2 2.5 concatenate.737
  677.2 4.2 collective-permute-start.55
  681.5 3.9 fusion.96
  690.8 2.5 broadcast_in_dim.759
  701.9 2.5 broadcast_in_dim.775
  710.7 3.2 collective-permute-start.57
  715.1 2.5 concatenate.817
  718.8 2.5 broadcast_in_dim.776
  727.5 2.5 broadcast_in_dim.779
  736.2 5.8 fusion.148
  (942 shorter events, 458.7 us)
Async XLA Ops:
  10.9 99.4 %all-to-all-start = ((f32[8,4,2,1024]{3,2,1,0:T(2,128)}), f32[8,4,2,1024]{3,2,1,0:T(2,128)}, u32[]{:S(2)}, u32[]{:S(2)}) async-start(f32[8,4,2,1024]{3,2,1,0:T(2,128)} %tile.12), calls=%async_computation | async-start | bytes 524288 | tf_op jit(solution)/shard_map/all_to_all | solution.py:16
  51.3 19.4 %collective-permute-start.2 = (f32[16,5,2]{2,0,1:T(8,128)}, f32[16,5,2]{2,0,1:T(8,128)}, u32[]{:S(2)}, u32[]{:S(2)}) collective-permute-start(f32[16,5,2]{2,0,1:T(8,128)} %broadcast_multiply_fusion.3), channel_id=1, source_target_pairs={{0,1},{1,0},{2,3},{3,2},{4,5},{5,4},{6,7},{7,6},{8,9},{9,8},{10,11... | collective-permute-start | bytes 1928 | tf_op jit(solution)/shard_map/ppermute | solution.py:204
  57.0 47.3 %collective-permute-start.1 = (f32[1,2,1024]{2,1,0:T(2,128)}, f32[1,2,1024]{2,1,0:T(2,128)}, u32[]{:S(2)}, u32[]{:S(2)}) collective-permute-start(f32[1,2,1024]{2,1,0:T(2,128)} %stack_reshape_squeeze.37), channel_id=1, source_target_pairs={{0,1},{1,2},{2,3},{3,4},{4,5},{5,6},{6,7},{7,8},{8,9},{9,10},{10,1... | collective-permute-start | bytes 24584 | tf_op jit(solution)/shard_map/ppermute | solution.py:24
  61.0 40.7 %collective-permute-start = (f32[1,2,1024]{2,1,0:T(2,128)}, f32[1,2,1024]{2,1,0:T(2,128)}, u32[]{:S(2)}, u32[]{:S(2)}) collective-permute-start(f32[1,2,1024]{2,1,0:T(2,128)} %stack_reshape_squeeze.36), channel_id=1, source_target_pairs={{1,0},{2,1},{3,2},{4,3},{5,4},{6,5},{7,6},{8,7},{9,8},{10,9},{11,1... | collective-permute-start | bytes 24584 | tf_op jit(solution)/shard_map/ppermute | solution.py:27
  71.6 7.5 %collective-permute-start.3 = (f32[16,5,2]{2,0,1:T(8,128)S(1)}, f32[16,5,2]{2,0,1:T(8,128)S(1)}, u32[]{:S(2)}, u32[]{:S(2)}) collective-permute-start(f32[16,5,2]{2,0,1:T(8,128)S(1)} %fusion.171), channel_id=1, source_target_pairs={{0,2},{1,3},{2,0},{3,1},{4,6},{5,7},{6,4},{7,5},{8,10},{9,11},{10,... | collective-permute-start | bytes 1928 | tf_op jit(solution)/shard_map/ppermute | solution.py:204
  80.0 5.6 collective-permute-start.4
  85.6 7.6 %collective-permute-start.5 = (f32[16,5,2]{2,0,1:T(8,128)S(1)}, f32[16,5,2]{2,0,1:T(8,128)S(1)}, u32[]{:S(2)}, u32[]{:S(2)}) collective-permute-start(f32[16,5,2]{2,0,1:T(8,128)S(1)} %add.671), channel_id=1, source_target_pairs={{0,8},{1,9},{2,10},{3,11},{4,12},{5,13},{6,14},{7,15},{8,0},{9,1},... | collective-permute-start | bytes 1928 | tf_op jit(solution)/shard_map/ppermute | solution.py:204
  150.2 32.0 %all-to-all-start.1 = ((f32[8,4,2,1024]{3,2,1,0:T(2,128)}), f32[8,4,2,1024]{3,2,1,0:T(2,128)}, u32[]{:S(2)}, u32[]{:S(2)}) async-start(f32[8,4,2,1024]{3,2,1,0:T(2,128)} %tile.13), calls=%async_computation.1 | async-start | bytes 524288 | tf_op jit(solution)/shard_map/all_to_all | solution.py:16
  157.9 12.6 %collective-permute-start.14 = (f32[1,2,1024]{2,1,0:T(2,128)}, f32[1,2,1024]{2,1,0:T(2,128)}, u32[]{:S(2)}, u32[]{:S(2)}) collective-permute-start(f32[1,2,1024]{2,1,0:T(2,128)} %stack_reshape_squeeze.39), channel_id=1, source_target_pairs={{0,1},{1,2},{2,3},{3,4},{4,5},{5,6},{6,7},{7,8},{8,9},{9,10},{10,1... | collective-permute-start | bytes 24584 | tf_op jit(solution)/shard_map/ppermute | solution.py:24
  159.8 16.6 %collective-permute-start.13 = (f32[1,2,1024]{2,1,0:T(2,128)}, f32[1,2,1024]{2,1,0:T(2,128)}, u32[]{:S(2)}, u32[]{:S(2)}) collective-permute-start(f32[1,2,1024]{2,1,0:T(2,128)} %stack_reshape_squeeze.38), channel_id=1, source_target_pairs={{1,0},{2,1},{3,2},{4,3},{5,4},{6,5},{7,6},{8,7},{9,8},{10,9},{11,1... | collective-permute-start | bytes 24584 | tf_op jit(solution)/shard_map/ppermute | solution.py:27
  198.6 1.3 collective-permute-start.15
  201.2 3.6 collective-permute-start.16
  204.8 5.1 collective-permute-start.17
  209.9 4.1 collective-permute-start.18
  213.9 5.1 collective-permute-start.19
  219.6 16.6 %collective-permute-start.20 = (f32[257]{0:T(512)}, f32[257]{0:T(512)}, u32[]{:S(2)}, u32[]{:S(2)}) collective-permute-start(f32[257]{0:T(512)} %add.700), channel_id=1, source_target_pairs={{0,4},{1,5},{2,6},{3,7},{4,0},{5,1},{6,2},{7,3},{8,12},{9,13},{10,... | collective-permute-start | bytes 3092 | tf_op jit(solution)/shard_map/ppermute | solution.py:204
  231.6 7.5 %collective-permute-start.6 = (f32[1]{0:T(128)}, f32[1]{0:T(128)}, u32[]{:S(2)}, u32[]{:S(2)}) collective-permute-start(f32[1]{0:T(128)} %bitcast.39), channel_id=1, source_target_pairs={{0,16},{16,0},{32,48},{48,32},{64,80},{80,64},{96,112},{112,96},{1... | collective-permute-start | bytes 20 | tf_op jit(solution)/shard_map/ppermute | solution.py:204
  237.0 34.4 %collective-permute-start.21 = (f32[257]{0:T(512)S(1)}, f32[257]{0:T(512)S(1)}, u32[]{:S(2)}, u32[]{:S(2)}) collective-permute-start(f32[257]{0:T(512)S(1)} %add.701), channel_id=1, source_target_pairs={{0,8},{1,9},{2,10},{3,11},{4,12},{5,13},{6,14},{7,15},{8,0},{9,1},... | collective-permute-start | bytes 3092 | tf_op jit(solution)/shard_map/ppermute | solution.py:204
  240.4 3.7 collective-permute-start.7
  244.7 5.2 collective-permute-start.8
  250.6 3.7 collective-permute-start.9
  254.9 5.2 collective-permute-start.10
  260.8 3.7 collective-permute-start.11
  265.1 5.6 collective-permute-start.12
  300.3 37.6 %all-to-all-start.2 = ((f32[8,4,2,1024]{3,2,1,0:T(2,128)}), f32[8,4,2,1024]{3,2,1,0:T(2,128)}, u32[]{:S(2)}, u32[]{:S(2)}) async-start(f32[8,4,2,1024]{3,2,1,0:T(2,128)} %tile.14), calls=%async_computation.2 | async-start | bytes 524288 | tf_op jit(solution)/shard_map/all_to_all | solution.py:16
  308.0 18.2 %collective-permute-start.23 = (f32[1,2,1024]{2,1,0:T(2,128)}, f32[1,2,1024]{2,1,0:T(2,128)}, u32[]{:S(2)}, u32[]{:S(2)}) collective-permute-start(f32[1,2,1024]{2,1,0:T(2,128)} %stack_reshape_squeeze.41), channel_id=1, source_target_pairs={{0,1},{1,2},{2,3},{3,4},{4,5},{5,6},{6,7},{7,8},{8,9},{9,10},{10,1... | collective-permute-start | bytes 24584 | tf_op jit(solution)/shard_map/ppermute | solution.py:24
  310.5 21.5 %collective-permute-start.22 = (f32[1,2,1024]{2,1,0:T(2,128)}, f32[1,2,1024]{2,1,0:T(2,128)}, u32[]{:S(2)}, u32[]{:S(2)}) collective-permute-start(f32[1,2,1024]{2,1,0:T(2,128)} %stack_reshape_squeeze.40), channel_id=1, source_target_pairs={{1,0},{2,1},{3,2},{4,3},{5,4},{6,5},{7,6},{8,7},{9,8},{10,9},{11,1... | collective-permute-start | bytes 24584 | tf_op jit(solution)/shard_map/ppermute | solution.py:27
  353.3 4.9 collective-permute-start.24
  359.5 3.7 collective-permute-start.25
  363.8 5.2 collective-permute-start.26
  369.7 4.1 collective-permute-start.27
  374.5 5.2 collective-permute-start.28
  380.3 5.5 collective-permute-start.29
  386.5 5.4 collective-permute-start.30
  408.0 24.3 %all-to-all-start.3 = ((f32[8,4,2,1024]{3,2,1,0:T(2,128)}), f32[8,4,2,1024]{3,2,1,0:T(2,128)}, u32[]{:S(2)}, u32[]{:S(2)}) async-start(f32[8,4,2,1024]{3,2,1,0:T(2,128)} %tile.15), calls=%async_computation.3 | async-start | bytes 524288 | tf_op jit(solution)/shard_map/all_to_all | solution.py:16
  413.6 11.2 %collective-permute-start.32 = (f32[1,2,1024]{2,1,0:T(2,128)S(1)}, f32[1,2,1024]{2,1,0:T(2,128)S(1)}, u32[]{:S(2)}, u32[]{:S(2)}) collective-permute-start(f32[1,2,1024]{2,1,0:T(2,128)S(1)} %stack_reshape_squeeze.43), channel_id=1, source_target_pairs={{0,1},{1,2},{2,3},{3,4},{4,5},{5,6},{6,7},{7,8},{8,9},{9,10},{10,1... | collective-permute-start | bytes 24584 | tf_op jit(solution)/shard_map/ppermute | solution.py:24
  415.8 12.0 %collective-permute-start.31 = (f32[1,2,1024]{2,1,0:T(2,128)}, f32[1,2,1024]{2,1,0:T(2,128)}, u32[]{:S(2)}, u32[]{:S(2)}) collective-permute-start(f32[1,2,1024]{2,1,0:T(2,128)} %stack_reshape_squeeze.42), channel_id=1, source_target_pairs={{1,0},{2,1},{3,2},{4,3},{5,4},{6,5},{7,6},{8,7},{9,8},{10,9},{11,1... | collective-permute-start | bytes 24584 | tf_op jit(solution)/shard_map/ppermute | solution.py:27
  439.8 1.2 collective-permute-start.33
  441.6 3.6 collective-permute-start.34
  445.2 5.1 collective-permute-start.35
  450.3 4.2 collective-permute-start.36
  454.5 5.4 collective-permute-start.37
  460.0 7.1 collective-permute-start.38
  467.7 12.5 %collective-permute-start.39 = (f32[257]{0:T(512)}, f32[257]{0:T(512)}, u32[]{:S(2)}, u32[]{:S(2)}) collective-permute-start(f32[257]{0:T(512)} %add.733), channel_id=1, source_target_pairs={{0,8},{1,9},{2,10},{3,11},{4,12},{5,13},{6,14},{7,15},{8,0},{9,1},... | collective-permute-start | bytes 3092 | tf_op jit(solution)/shard_map/ppermute | solution.py:204
  504.2 35.7 %all-to-all-start.4 = ((f32[8,4,2,1024]{3,2,1,0:T(2,128)}), f32[8,4,2,1024]{3,2,1,0:T(2,128)}, u32[]{:S(2)}, u32[]{:S(2)}) async-start(f32[8,4,2,1024]{3,2,1,0:T(2,128)} %tile.16), calls=%async_computation.4 | async-start | bytes 524288 | tf_op jit(solution)/shard_map/all_to_all | solution.py:16
  511.3 17.6 %collective-permute-start.41 = (f32[1,2,1024]{2,1,0:T(2,128)S(1)}, f32[1,2,1024]{2,1,0:T(2,128)S(1)}, u32[]{:S(2)}, u32[]{:S(2)}) collective-permute-start(f32[1,2,1024]{2,1,0:T(2,128)S(1)} %stack_reshape_squeeze.45), channel_id=1, source_target_pairs={{0,1},{1,2},{2,3},{3,4},{4,5},{5,6},{6,7},{7,8},{8,9},{9,10},{10,1... | collective-permute-start | bytes 24584 | tf_op jit(solution)/shard_map/ppermute | solution.py:24
  513.2 20.9 %collective-permute-start.40 = (f32[1,2,1024]{2,1,0:T(2,128)}, f32[1,2,1024]{2,1,0:T(2,128)}, u32[]{:S(2)}, u32[]{:S(2)}) collective-permute-start(f32[1,2,1024]{2,1,0:T(2,128)} %stack_reshape_squeeze.44), channel_id=1, source_target_pairs={{1,0},{2,1},{3,2},{4,3},{5,4},{6,5},{7,6},{8,7},{9,8},{10,9},{11,1... | collective-permute-start | bytes 24584 | tf_op jit(solution)/shard_map/ppermute | solution.py:27
  555.6 4.8 collective-permute-start.42
  561.7 3.6 collective-permute-start.43
  565.9 5.1 collective-permute-start.44
  571.6 4.0 collective-permute-start.45
  576.2 5.1 collective-permute-start.46
  581.9 6.1 collective-permute-start.47
  588.6 5.1 collective-permute-start.48
  613.4 21.8 %all-to-all-start.5 = ((f32[8,4,2,1024]{3,2,1,0:T(2,128)}), f32[8,4,2,1024]{3,2,1,0:T(2,128)}, u32[]{:S(2)}, u32[]{:S(2)}) async-start(f32[8,4,2,1024]{3,2,1,0:T(2,128)} %tile.17), calls=%async_computation.5 | async-start | bytes 524288 | tf_op jit(solution)/shard_map/all_to_all | solution.py:16
  618.4 10.3 %collective-permute-start.50 = (f32[1,2,1024]{2,1,0:T(2,128)S(1)}, f32[1,2,1024]{2,1,0:T(2,128)S(1)}, u32[]{:S(2)}, u32[]{:S(2)}) collective-permute-start(f32[1,2,1024]{2,1,0:T(2,128)S(1)} %stack_reshape_squeeze.47), channel_id=1, source_target_pairs={{0,1},{1,2},{2,3},{3,4},{4,5},{5,6},{6,7},{7,8},{8,9},{9,10},{10,1... | collective-permute-start | bytes 24584 | tf_op jit(solution)/shard_map/ppermute | solution.py:24
  620.3 11.1 %collective-permute-start.49 = (f32[1,2,1024]{2,1,0:T(2,128)S(1)}, f32[1,2,1024]{2,1,0:T(2,128)S(1)}, u32[]{:S(2)}, u32[]{:S(2)}) collective-permute-start(f32[1,2,1024]{2,1,0:T(2,128)S(1)} %stack_reshape_squeeze.46), channel_id=1, source_target_pairs={{1,0},{2,1},{3,2},{4,3},{5,4},{6,5},{7,6},{8,7},{9,8},{10,9},{11,1... | collective-permute-start | bytes 24584 | tf_op jit(solution)/shard_map/ppermute | solution.py:27
  643.9 1.2 collective-permute-start.51
  645.8 3.6 collective-permute-start.52
  649.4 5.1 collective-permute-start.53
  654.5 22.7 %collective-permute-start.54 = (f32[257]{0:T(512)S(1)}, f32[257]{0:T(512)S(1)}, u32[]{:S(2)}, u32[]{:S(2)}) collective-permute-start(f32[257]{0:T(512)S(1)} %add.758), channel_id=1, source_target_pairs={{0,1},{1,0},{2,3},{3,2},{4,5},{5,4},{6,7},{7,6},{8,9},{9,8},{10,11... | collective-permute-start | bytes 3092 | tf_op jit(solution)/shard_map/ppermute | solution.py:204
  677.2 8.1 %collective-permute-start.55 = (f32[257]{0:T(512)S(1)}, f32[257]{0:T(512)S(1)}, u32[]{:S(2)}, u32[]{:S(2)}) collective-permute-start(f32[257]{0:T(512)S(1)} %add.759), channel_id=1, source_target_pairs={{0,2},{1,3},{2,0},{3,1},{4,6},{5,7},{6,4},{7,5},{8,10},{9,11},{10,... | collective-permute-start | bytes 3092 | tf_op jit(solution)/shard_map/ppermute | solution.py:204
  685.9 23.5 %collective-permute-start.56 = (f32[257]{0:T(512)}, f32[257]{0:T(512)}, u32[]{:S(2)}, u32[]{:S(2)}) collective-permute-start(f32[257]{0:T(512)} %add.760), channel_id=1, source_target_pairs={{0,4},{1,5},{2,6},{3,7},{4,0},{5,1},{6,2},{7,3},{8,12},{9,13},{10,... | collective-permute-start | bytes 3092 | tf_op jit(solution)/shard_map/ppermute | solution.py:204
  710.7 23.5 %collective-permute-start.57 = (f32[257]{0:T(512)}, f32[257]{0:T(512)}, u32[]{:S(2)}, u32[]{:S(2)}) collective-permute-start(f32[257]{0:T(512)} %add.761), channel_id=1, source_target_pairs={{0,8},{1,9},{2,10},{3,11},{4,12},{5,13},{6,14},{7,15},{8,0},{9,1},... | collective-permute-start | bytes 3092 | tf_op jit(solution)/shard_map/ppermute | solution.py:204
  (217 other events, 1722.2 us)
